TPU v7x, 32 devices: a whole 2x2x4 slice. The times are simulated.
32 devices in a mesh: guide: 2 (over core), blk: 16 (over z, y, x).
Axes of the slice: x: 2, y: 2, z: 4, core: 2. Of those that a mesh axis runs over, the one named last changes fastest.
Arguments:
- x_cols: bfloat16 [128, 2048], P(None, 'blk'), may hold values from -3 to 3
- queries: bfloat16 [128, 9216], P('blk'), may hold values from -64 to 64
- new_kv: bfloat16 [128, 576], P('blk'), may hold values from -6 to 6
- cache: bfloat16 [2, 128, 256, 576], P('guide', 'blk'), may hold values from -8 to 8
- lengths: int32 [2, 128], P('guide'), may hold values from 2 to 256, as said below
- perm: int32 [128], replicated, may hold values from 0 to 127, each once
- guide_scale: float32 [128], replicated, may hold values from 1.5 to 7.5
- w_uv: bfloat16 [16, 512, 128], replicated, may hold values from -0.75 to 0.75
- w_out: bfloat16 [2048, 2048], P(None, 'blk'), may hold values from -0.125 to 0.125
- mlp_gain: float32 [2048], replicated, may hold values from 0.5 to 1.5
- w_gate: bfloat16 [2048, 10944], P(None, 'blk'), may hold values from -0.125 to 0.125
- w_up: bfloat16 [2048, 10944], P(None, 'blk'), may hold values from -0.125 to 0.125
- w_down: bfloat16 [10944, 2048], P('blk'), may hold values from -0.0546875 to 0.0546875
- head_gain: float32 [2048], replicated, may hold values from 0.5 to 1.5
- w_head: bfloat16 [2048, 102400], P(None, 'blk'), may hold values from -0.125 to 0.125
Outputs:
- guided: bfloat16 [128, 102400], P('guide', 'blk')
Inputs may be any that keep to these rules, and one draw needn't show every extreme that they name: Positions 0 to lengths[g, r] - 1 of request r's cache in group g are live; each group has a request with 256 live positions. Slot s holds request perm[s]; every request has one slot.
All inputs are finite; a program needn't handle non-finite values.
Results may differ from a plain program's by a relative error of at most 0.018.
Values may be sent and summed in bfloat16 or wider, within the bound.
No kernel may reach another device: no remote copies, remote signals or barrier semaphores. Data moves between devices by JAX's collectives and lax.ppermute only.
A program may use at most 128 MiB of HBM per device.

v0:
```python
import jax
import jax.numpy as jnp
from jax import lax
from jax.sharding import PartitionSpec as P

FF = 10944


def partner(value, axis, apart):
    mask = 2**apart
    pairs = [(source, source ^ mask) for source in range(lax.axis_size(axis))]
    return lax.ppermute(value, axis, pairs)


def rms_round(hidden, gain):
    values = hidden.astype(jnp.float32)
    meansq = jnp.mean(values * values, axis=-1, keepdims=True)
    return (values * lax.rsqrt(meansq + 1e-06) * gain).astype(jnp.bfloat16)


def body(
    x_cols,
    queries,
    new_kv,
    cache,
    lengths,
    perm,
    guide_scale,
    w_uv,
    w_out,
    mlp_gain,
    w_gate,
    w_up,
    w_down,
    head_gain,
    w_head,
):
    guide_index = lax.axis_index("guide")
    blk_index = lax.axis_index("blk")
    slots_dev = queries.shape[0]
    heads_count = w_uv.shape[0]
    latent_size = w_uv.shape[1]
    key_width = new_kv.shape[1]
    score_scale = (w_uv.shape[2] + key_width - latent_size) ** (-0.5)
    slot_ids = blk_index * slots_dev + jnp.arange(slots_dev, dtype=jnp.int32)
    owners = jnp.take(perm, slot_ids)
    live_len = jnp.take(lengths[0], owners)
    query_heads = queries.reshape(slots_dev, heads_count, key_width)
    cached_keys = cache[0]
    scores = (
        jnp.einsum("shk,slk->shl", query_heads, cached_keys, preferred_element_type=jnp.float32)
        * score_scale
    )
    own_score = (
        jnp.einsum("shk,sk->sh", query_heads, new_kv, preferred_element_type=jnp.float32)
        * score_scale
    )
    live_mask = (
        jnp.arange(cached_keys.shape[1], dtype=jnp.int32)[None, None, :] < live_len[:, None, None]
    )
    scores = jnp.where(live_mask, scores, jnp.float32(-1e30))
    peak_score = jnp.maximum(jnp.max(scores, axis=-1), own_score)
    probs = jnp.where(live_mask, jnp.exp(scores - peak_score[..., None]), jnp.float32(0.0))
    own_prob = jnp.exp(own_score - peak_score)
    softmax_total = jnp.sum(probs, axis=-1) + own_prob
    weights = (probs / softmax_total[..., None]).astype(jnp.bfloat16)
    own_weight = (own_prob / softmax_total).astype(jnp.bfloat16)
    latent_out = jnp.einsum(
        "shl,slc->shc", weights, cached_keys[:, :, :latent_size], preferred_element_type=jnp.float32
    )
    latent_out = latent_out + own_weight.astype(jnp.float32)[..., None] * new_kv[
        :, None, :latent_size
    ].astype(jnp.float32)
    value_rows = jnp.einsum(
        "shc,hcd->shd", latent_out.astype(jnp.bfloat16), w_uv, preferred_element_type=jnp.float32
    )
    value_rows = value_rows.astype(jnp.bfloat16).reshape(slots_dev, -1)
    attended = jnp.dot(
        lax.all_gather(value_rows, "blk", axis=0, tiled=True),
        w_out,
        preferred_element_type=jnp.float32,
    )
    residual = (x_cols.astype(jnp.float32) + attended).astype(jnp.bfloat16)
    rows_full = lax.all_gather(residual, "blk", axis=1, tiled=True)
    normed = rms_round(rows_full, mlp_gain)
    unit_count = w_gate.shape[1]
    gate_out = jnp.dot(normed, w_gate, preferred_element_type=jnp.float32)
    up_out = jnp.dot(normed, w_up, preferred_element_type=jnp.float32)
    unit_ids = blk_index * unit_count + jnp.arange(unit_count, dtype=jnp.int32)
    hidden = jnp.where(
        unit_ids[None, :] < FF, jax.nn.silu(gate_out) * up_out, jnp.float32(0.0)
    ).astype(jnp.bfloat16)
    partial_sum = jnp.dot(hidden, w_down, preferred_element_type=jnp.float32)
    summed = lax.psum(partial_sum, "blk")
    after_mlp = (rows_full.astype(jnp.float32) + summed).astype(jnp.bfloat16)
    logits = jnp.dot(rms_round(after_mlp, head_gain), w_head, preferred_element_type=jnp.float32)
    request_count = logits.shape[0]
    half_rows = request_count // 2
    slot_scale = jnp.take(guide_scale, perm)
    request_order = (
        jnp.zeros((request_count,), jnp.int32)
        .at[perm]
        .set(jnp.arange(request_count, dtype=jnp.int32))
    )
    own_order = lax.dynamic_slice_in_dim(request_order, guide_index * half_rows, half_rows)
    other_logits = partner(logits.astype(jnp.bfloat16), "guide", 0).astype(logits.dtype)
    cond_logits = jnp.where(guide_index == 0, logits, other_logits)
    uncond_logits = jnp.where(guide_index == 0, other_logits, logits)
    mixed = (uncond_logits + slot_scale[:, None] * (cond_logits - uncond_logits)).astype(
        jnp.bfloat16
    )
    return jnp.take(mixed, own_order, axis=0)


def solution(mesh):
    return jax.shard_map(
        body,
        mesh=mesh,
        in_specs=(
            P(None, "blk"),
            P("blk", None),
            P("blk", None),
            P("guide", "blk", None, None),
            P("guide", None),
            P(),
            P(),
            P(),
            P(None, "blk"),
            P(),
            P(None, "blk"),
            P(None, "blk"),
            P("blk", None),
            P(),
            P(None, "blk"),
        ),
        out_specs=P("guide", "blk"),
        check_vma=False,
    )
```

profile of v0, /device:TPU:0, one launch (start us, length us, event | category | flops | bytes accessed | tf_op | source)
XLA Modules:
  0.0 257.7 jit_solution(10083849745343940406)
XLA Ops:
  6.5 1.2 reshape.73
  7.8 1.3 gather_fusion.2
  9.1 1.3 gather_fusion.3
  10.5 0.7 slice_convert_fusion
  11.2 0.9 fusion.44
  12.1 2.2 fusion.55
  14.3 0.2 fusion.39
  14.6 2.4 fusion.4
  17.0 0.5 fusion.11
  17.5 45.3 %all_gather.6 = bf16[128,2048]{1,0:T(8,128)(2,1)S(1)} all-gather(bf16[8,2048]{1,0:T(8,128)(2,1)S(1)} %fusion.11), channel_id=1, replica_groups=mesh['guide'=2,'blk'=16] {'blk'}, dimensions={0}, use_global_device_ids=true | all-gather | bytes 557056 | tf_op jit(solution)/shard_map/all_gather | solution.py:79
  62.8 0.3 fusion.10
  63.1 38.5 %all_gather.7 = bf16[128,2048]{1,0:T(8,128)(2,1)S(1)} all-gather(bf16[128,128]{1,0:T(8,128)(2,1)S(1)} %fusion.10), channel_id=1, replica_groups=mesh['guide'=2,'blk'=16] {'blk'}, dimensions={1}, use_global_device_ids=true | all-gather | bytes 557056 | tf_op jit(solution)/shard_map/all_gather | solution.py:84
  101.7 0.2 fusion.15
  101.9 3.5 %fusion.34 = f32[128,684]{0,1:T(8,128)} fusion(bf16[2048,684]{0,1:T(8,128)(2,1)} %param.27, bf16[128,2048]{1,0:T(8,128)(2,1)S(1)} %all_gather.7, f32[2048]{0:T(1024)S(1)} %copy-done.7, f32[128]{0:T(128)S(1)} %add_rsqrt_fusion.1), kind=kOutput, calls=%fused_computation.49 | convolution fusion | flops 359661568 | bytes 3684864 | tf_op jit(solution)/shard_map/dot_general | solution.py:87
  105.4 5.0 %fusion.8 = f32[128,2048]{1,0:T(8,128)} fusion(bf16[684,2048]{1,0:T(8,128)(2,1)S(1)} %copy-done, bf16[2048,684]{0,1:T(8,128)(2,1)} %param.28, f32[128,684]{0,1:T(8,128)} %fusion.34, pred[684]{0:T(1024)(128)(4,1)S(1)} %add_compare_fusion, bf16[128,2048]{1,0:T(8,128)(2,1)S(1)} %all_gather.7, f32[2048]{0:T(1024)S(1)} %copy-done.7, f32[128]{0:T(128)S(1)} %add_rsqrt_fusion.1), kind=kOutput, calls=%fused_computation.21 | convolution fusion | flops 718887424 | bytes 7535788 | tf_op jit(solution)/shard_map/dot_general | solution.py:93
  110.5 109.6 %all-reduce.2.cloned.1.call-done = f32[128,2048]{1,0:T(8,128)} async-done(((f32[128,2048]{1,0:T(8,128)}), f32[128,2048]{1,0:T(8,128)}) %all-reduce.2.cloned.1.call-update) | async-done | bytes 1048592 | tf_op jit(solution)/shard_map/psum | solution.py:94
  220.1 1.4 fusion.12
  221.5 14.7 %fusion.56 = (bf16[128,6400]{1,0:T(8,128)(2,1)}, f32[128,6400]{1,0:T(8,128)}) fusion(bf16[2048,6400]{1,0:T(8,128)(2,1)} %param.31, f32[2048]{0:T(1024)S(1)} %copy-done.5, f32[128]{0:T(128)S(1)} %add_rsqrt_fusion, f32[128,2048]{1,0:T(8,128)} %all-reduce.2.cloned.1.call-done, bf16[128,2048]{1,0:T(8,128)(2,1)S(1)} %all_gather.7), kind=kOutput, calls=%fused_computation.90 | convolution fusion | flops 3358097408 | bytes 32711168 | tf_op jit(solution)/shard_map/dot_general | solution.py:96
  236.2 1.2 scatter_custom_fusion
  237.4 1.2 gather_fusion
  238.8 1.3 collective-permute-done
  240.1 4.3 %fusion.3 = bf16[128,6400]{1,0:T(8,128)(2,1)} fusion(f32[128,6400]{1,0:T(8,128)} %get-tuple-element.13, bf16[128,6400]{1,0:T(8,128)(2,1)} %collective-permute-done, f32[128]{0:T(128)S(1)} %and_select_fusion.2, pred[]{:T(512)S(6)} %eq.4), kind=kLoop, calls=%fused_computation.10 | loop fusion | flops 5734400 | bytes 6554113 | tf_op jit(solution)/shard_map/convert_element_type | solution.py:109
  244.4 4.3 %gather_fusion.1 = bf16[64,6400]{1,0:T(8,128)(2,1)} fusion(bf16[128,6400]{1,0:T(8,128)(2,1)} %fusion.3, s32[1024]{0:T(1024)S(1)} %pad_clamp_fusion), kind=kCustom, calls=%fused_computation.3 | custom fusion | bytes 1638656 | tf_op jit(solution)/shard_map/jit(_take)/gather | solution.py:112
  248.7 2.2 broadcast_select_fusion
  (37 shorter events, 0.4 us)
Async XLA Ops:
  6.5 98.9 %copy-start = (bf16[684,2048]{1,0:T(8,128)(2,1)S(1)}, bf16[684,2048]{1,0:T(8,128)(2,1)}, u32[]{:S(2)}) copy-start(bf16[684,2048]{1,0:T(8,128)(2,1)} %param.29) | copy-start | bytes 8404996
  6.5 213.5 %all-reduce.2.cloned.1.call-start = ((), (), s32[]{:S(2)}) async-start(), calls=%async_computation | async-start | bytes 2097152 | tf_op jit(solution)/shard_map/psum | solution.py:94
  14.6 2.4 copy-start.3
  14.6 48.3 %copy-start.4 = (bf16[2048,128]{1,0:T(8,128)(2,1)S(1)}, bf16[2048,128]{1,0:T(8,128)(2,1)}, u32[]{:S(2)}) copy-start(bf16[2048,128]{1,0:T(8,128)(2,1)} %param.25) | copy-start | bytes 1572868
  14.6 48.3 %copy-start.6 = (bf16[128,128]{1,0:T(8,128)(2,1)S(1)}, bf16[128,128]{1,0:T(8,128)(2,1)}, u32[]{:S(2)}) copy-start(bf16[128,128]{1,0:T(8,128)(2,1)} %param.17) | copy-start | bytes 98308
  17.0 84.9 %copy-start.7 = (f32[2048]{0:T(1024)S(1)}, f32[2048]{0:T(1024)}, u32[]{:S(2)}) copy-start(f32[2048]{0:T(1024)} %param.26) | copy-start | bytes 24580
  105.4 116.1 %copy-start.5 = (f32[2048]{0:T(1024)S(1)}, f32[2048]{0:T(1024)}, u32[]{:S(2)}) copy-start(f32[2048]{0:T(1024)} %param.30) | copy-start | bytes 24580
  221.5 14.7 %copy-start.2 = (s32[128]{0:T(128)S(1)}, s32[128]{0:T(128)}, u32[]{:S(2)}) copy-start(s32[128]{0:T(128)} %param.22) | copy-start | bytes 1540
  221.5 15.9 %copy-start.1 = (f32[128]{0:T(128)S(1)}, f32[128]{0:T(128)}, u32[]{:S(2)}) copy-start(f32[128]{0:T(128)} %param.23) | copy-start | bytes 1540
  236.2 3.8 %collective-permute-start = (bf16[128,6400]{1,0:T(8,128)(2,1)}, bf16[128,6400]{1,0:T(8,128)(2,1)}, u32[]{:S(2)}, u32[]{:S(2)}) collective-permute-start(bf16[128,6400]{1,0:T(8,128)(2,1)} %get-tuple-element.12), channel_id=1, source_target_pairs={{0,16},{16,0},{1,17},{17,1},{2,18},{18,2},{3,19},{19,3},{4,20},{20... | collective-permute-start | bytes 4915208 | tf_op jit(solution)/shard_map/ppermute | solution.py:12
Sparse Core Ops, SparseCore 0:
  110.6 109.4 all-reduce.1
where the time goes:
time: 258 us
  waiting for transfers between devices  111 us (43%)
  blocking collectives  83.9 us (33%)
  matrix products  29.5 us (11%)
  between operations  13.5 us (5%)
  local copies, waits for them, and re-layouts  10.7 us (4%)
  other arithmetic  9.26 us (4%)
    psum x1, waiting for transfers between devices, body(): summed = lax.psum(partial_sum, 'blk')  110 us
    all_gather x1, blocking collectives, body(): lax.all_gather(value_rows, 'blk', axis=0, tiled=True)  45.3 us
    all_gather x1, blocking collectives, body(): rows_full = lax.all_gather(residual, 'blk', axis=1, tiled=True)  38.5 us
    dot_general x1, matrix products, body(): jnp.dot(rms_round(after_mlp, head_gain), w_head, preferred_element_type=j...  14.7 us
  transfers between devices with their start and end apart: 2, of which 2 were waited for; matrix products, arithmetic and copies ran while one was open for 1% of the time, Pallas kernels for 0%

commit v1 on v0

--- a/solution.py
+++ b/solution.py
@@ -91,7 +91,9 @@
         unit_ids[None, :] < FF, jax.nn.silu(gate_out) * up_out, jnp.float32(0.0)
     ).astype(jnp.bfloat16)
     partial_sum = jnp.dot(hidden, w_down, preferred_element_type=jnp.float32)
-    summed = lax.psum(partial_sum, "blk")
+    summed = partial_sum
+    for hop in (1, 2, 4, 8):
+        summed = summed + lax.ppermute(summed, "blk", [(dev, dev ^ hop) for dev in range(16)])
     after_mlp = (rows_full.astype(jnp.float32) + summed).astype(jnp.bfloat16)
     logits = jnp.dot(rms_round(after_mlp, head_gain), w_head, preferred_element_type=jnp.float32)
     request_count = logits.shape[0]

time: 258 us -> 217 us (0.84)
  waiting for transfers between devices: 111 us -> 80 us
  between operations: 13.5 us -> 0.23 us
    psum x1 -> x0, waiting for transfers between devices: 110 us -> none  [body(): summed = lax.psum(partial_sum, 'blk')]
    ppermute x0 -> x4, waiting for transfers between devices: none -> 78.7 us  [body(): lax.ppermute(summed, 'blk', [(dev, dev ^ hop) for dev in range(16)])]
  transfers between devices with their start and end apart: 2 -> 5, of which waited for: 2 -> 5; matrix products, arithmetic and copies ran while one was open for 1% -> 1% of each run, Pallas kernels for 0% -> 0%
where the time goes in v1:
time: 217 us; the launch traced here: 216 us
  blocking collectives  84 us (39%)
  waiting for transfers between devices  80 us (37%)
  matrix products  29.1 us (13%)
  local copies, waits for them, and re-layouts  10.7 us (5%)
  other arithmetic  9.78 us (5%)
  starting transfers between devices  2.43 us (1%)
    ppermute x4, waiting for transfers between devices, body(): lax.ppermute(summed, 'blk', [(dev, dev ^ hop) for dev in range(16)])  78.7 us
    all_gather x1, blocking collectives, body(): lax.all_gather(value_rows, 'blk', axis=0, tiled=True)  45.3 us
    all_gather x1, blocking collectives, body(): rows_full = lax.all_gather(residual, 'blk', axis=1, tiled=True)  38.7 us
    dot_general x1, matrix products, body(): jnp.dot(rms_round(after_mlp, head_gain), w_head, preferred_element_type=j...  14.3 us
    dot_general x1, matrix products, body(): partial_sum = jnp.dot(hidden, w_down, preferred_element_type=jnp.float32)  5.01 us
    convert_element_type x1, other arithmetic, body(): (uncond_logits + slot_scale[:, None] * (cond_logits - uncond_logits)).ast...  4.36 us
    gather x1, local copies, waits for them, and re-layouts, body(): return jnp.take(mixed, own_order, axis=0)  4.35 us
  transfers between devices with their start and end apart: 5, of which 5 were waited for; matrix products, arithmetic and copies ran while one was open for 1% of the time, Pallas kernels for 0%

profile of v1, /device:TPU:0, one launch (start us, length us, event | category | flops | bytes accessed | tf_op | source)
XLA Modules:
  0.0 216.3 jit_solution(16089499453523218442)
XLA Ops:
  0.0 1.2 reshape.73
  1.3 1.3 gather_fusion.2
  2.6 1.3 gather_fusion.3
  4.0 0.7 slice_convert_fusion
  4.7 0.9 fusion.44
  5.5 2.2 %fusion.55 = (f32[8,16]{1,0:T(8,128)S(1)}, f32[8,16,256]{2,1,0:T(8,128)S(1)}) fusion(bf16[8,16,576]{2,1,0:T(8,128)(2,1)S(1)} %reshape.73, bf16[1,8,256,576]{2,3,1,0:T(8,128)(2,1)} %param.20, pred[8,256]{1,0:T(8,128)(4,1)S(1)} %iota_compare_fusion), kind=kOutput, calls=%fused_computation.89 | convolution fusion | flops 37846912 | bytes 2640384 | tf_op jit(solution)/shard_map/shk,slk->shl/dot_general | solution.py:51
  8.0 2.4 %fusion.4 = f32[8,16,512]{2,1,0:T(8,128)S(1)} fusion(bf16[8,256,576]{1,2,0:T(8,128)(2,1)} %bitcast.23, f32[8,16,256]{2,1,0:T(8,128)S(1)} %get-tuple-element.13, f32[8,16]{1,0:T(8,128)S(1)} %get-tuple-element.11, f32[8,16]{1,0:T(8,128)S(1)} %multiply_maximum_fusion, pred[8,256]{1,0:T(8,128)(4,1)S(1)} %iota_compare_fusion), kind=kOutput, calls=%fused_computation.11 | convolution fusion | flops 33685504 | bytes 2493440 | tf_op jit(solution)/shard_map/shl,slc->shc/dot_general | solution.py:68
  11.0 45.3 %all_gather.6 = bf16[128,2048]{1,0:T(8,128)(2,1)S(1)} all-gather(bf16[8,2048]{1,0:T(8,128)(2,1)S(1)} %fusion.11), channel_id=1, replica_groups=mesh['guide'=2,'blk'=16] {'blk'}, dimensions={0}, use_global_device_ids=true | all-gather | bytes 557056 | tf_op jit(solution)/shard_map/all_gather | solution.py:79
  56.6 38.7 %all_gather.7 = bf16[128,2048]{1,0:T(8,128)(2,1)S(1)} all-gather(bf16[128,128]{1,0:T(8,128)(2,1)S(1)} %fusion.10), channel_id=1, replica_groups=mesh['guide'=2,'blk'=16] {'blk'}, dimensions={1}, use_global_device_ids=true | all-gather | bytes 557056 | tf_op jit(solution)/shard_map/all_gather | solution.py:84
  95.5 3.5 %fusion.34 = f32[128,684]{0,1:T(8,128)} fusion(bf16[2048,684]{0,1:T(8,128)(2,1)} %param.27, bf16[128,2048]{1,0:T(8,128)(2,1)S(1)} %all_gather.7, f32[2048]{0:T(1024)S(1)} %copy-done.7, f32[128]{0:T(128)S(1)} %add_rsqrt_fusion.1), kind=kOutput, calls=%fused_computation.49 | convolution fusion | flops 359661568 | bytes 3684864 | tf_op jit(solution)/shard_map/dot_general | solution.py:87
  99.0 5.0 %fusion.8 = f32[128,2048]{1,0:T(8,128)} fusion(bf16[684,2048]{1,0:T(8,128)(2,1)S(1)} %copy-done, bf16[2048,684]{0,1:T(8,128)(2,1)} %param.28, f32[128,684]{0,1:T(8,128)} %fusion.34, pred[684]{0:T(1024)(128)(4,1)S(1)} %add_compare_fusion, bf16[128,2048]{1,0:T(8,128)(2,1)S(1)} %all_gather.7, f32[2048]{0:T(1024)S(1)} %copy-done.7, f32[128]{0:T(128)S(1)} %add_rsqrt_fusion.1), kind=kOutput, calls=%fused_computation.21 | convolution fusion | flops 718887424 | bytes 7535788 | tf_op jit(solution)/shard_map/dot_general | solution.py:93
  104.0 2.2 %collective-permute-start = (f32[128,2048]{1,0:T(8,128)}, f32[128,2048]{1,0:T(8,128)S(1)}, u32[]{:S(2)}, u32[]{:S(2)}) collective-permute-start(f32[128,2048]{1,0:T(8,128)} %fusion.8), channel_id=1, source_target_pairs={{0,1},{1,0},{2,3},{3,2},{4,5},{5,4},{6,7},{7,6},{8,9},{9,8},{10,11... | collective-permute-start | bytes 3145736 | tf_op jit(solution)/shard_map/ppermute | solution.py:96
  106.2 13.0 %collective-permute-done = f32[128,2048]{1,0:T(8,128)S(1)} collective-permute-done((f32[128,2048]{1,0:T(8,128)}, f32[128,2048]{1,0:T(8,128)S(1)}, u32[]{:S(2)}, u32[]{:S(2)}) %collective-permute-start) | collective-permute-done | bytes 1048608 | tf_op jit(solution)/shard_map/ppermute | solution.py:96
  119.2 1.3 add.101
  120.6 14.8 %collective-permute-done.1 = f32[128,2048]{1,0:T(8,128)S(1)} collective-permute-done((f32[128,2048]{1,0:T(8,128)S(1)}, f32[128,2048]{1,0:T(8,128)S(1)}, u32[]{:S(2)}, u32[]{:S(2)}) %collective-permute-start.1) | collective-permute-done | bytes 1048608 | tf_op jit(solution)/shard_map/ppermute | solution.py:96
  135.6 25.1 %collective-permute-done.2 = f32[128,2048]{1,0:T(8,128)S(1)} collective-permute-done((f32[128,2048]{1,0:T(8,128)S(1)}, f32[128,2048]{1,0:T(8,128)S(1)}, u32[]{:S(2)}, u32[]{:S(2)}) %collective-permute-start.2) | collective-permute-done | bytes 1048608 | tf_op jit(solution)/shard_map/ppermute | solution.py:96
  160.9 25.9 %collective-permute-done.3 = f32[128,2048]{1,0:T(8,128)S(1)} collective-permute-done((f32[128,2048]{1,0:T(8,128)S(1)}, f32[128,2048]{1,0:T(8,128)S(1)}, u32[]{:S(2)}, u32[]{:S(2)}) %collective-permute-start.3) | collective-permute-done | bytes 1048608 | tf_op jit(solution)/shard_map/ppermute | solution.py:96
  187.2 14.3 %fusion.56 = (bf16[128,6400]{1,0:T(8,128)(2,1)}, f32[128,6400]{1,0:T(8,128)}) fusion(bf16[2048,6400]{1,0:T(8,128)(2,1)} %param.31, bf16[128,2048]{1,0:T(8,128)(2,1)S(1)} %get-tuple-element.9, f32[2048]{0:T(1024)S(1)} %copy-done.5, f32[128]{0:T(128)S(1)} %add_rsqrt_fusion), kind=kOutput, calls=%fused_computation.90 | convolution fusion | flops 3357310976 | bytes 31662592 | tf_op jit(solution)/shard_map/dot_general | solution.py:98
  201.6 1.2 scatter_custom_fusion
  202.8 1.2 gather_fusion
  204.1 1.3 collective-permute-done.4
  205.4 4.4 %fusion.3 = bf16[128,6400]{1,0:T(8,128)(2,1)} fusion(f32[128,6400]{1,0:T(8,128)} %get-tuple-element.15, bf16[128,6400]{1,0:T(8,128)(2,1)} %collective-permute-done.4, f32[128]{0:T(128)S(1)} %and_select_fusion.2, pred[]{:T(512)S(6)} %eq.4), kind=kLoop, calls=%fused_computation.10 | loop fusion | flops 5734400 | bytes 6554113 | tf_op jit(solution)/shard_map/convert_element_type | solution.py:111
  209.8 4.3 %gather_fusion.1 = bf16[64,6400]{1,0:T(8,128)(2,1)} fusion(bf16[128,6400]{1,0:T(8,128)(2,1)} %fusion.3, s32[1024]{0:T(1024)S(1)} %pad_clamp_fusion), kind=kCustom, calls=%fused_computation.3 | custom fusion | bytes 1638656 | tf_op jit(solution)/shard_map/jit(_take)/gather | solution.py:114
  214.1 2.2 %broadcast_select_fusion = bf16[64,6400]{1,0:T(8,128)(2,1)} fusion(bf16[64,6400]{1,0:T(8,128)(2,1)} %gather_fusion.1, pred[64]{0:T(512)(128)(4,1)S(1)} %get-tuple-element.6), kind=kLoop, calls=%fused_computation.35 | loop fusion | flops 409600 | bytes 1638464 | tf_op jit(solution)/shard_map/jit(_take)/select_n | solution.py:114
  (45 shorter events, 2.4 us)
Async XLA Ops:
  0.0 99.0 %copy-start = (bf16[684,2048]{1,0:T(8,128)(2,1)S(1)}, bf16[684,2048]{1,0:T(8,128)(2,1)}, u32[]{:S(2)}) copy-start(bf16[684,2048]{1,0:T(8,128)(2,1)} %param.29) | copy-start | bytes 8404996
  8.0 2.4 %copy-start.3 = (bf16[16,512,128]{2,1,0:T(8,128)(2,1)S(1)}, bf16[16,512,128]{2,1,0:T(8,128)(2,1)}, u32[]{:S(2)}) copy-start(bf16[16,512,128]{2,1,0:T(8,128)(2,1)} %param.24) | copy-start | bytes 6291460
  8.0 48.3 %copy-start.4 = (bf16[2048,128]{1,0:T(8,128)(2,1)S(1)}, bf16[2048,128]{1,0:T(8,128)(2,1)}, u32[]{:S(2)}) copy-start(bf16[2048,128]{1,0:T(8,128)(2,1)} %param.25) | copy-start | bytes 1572868
  8.0 48.3 %copy-start.6 = (bf16[128,128]{1,0:T(8,128)(2,1)S(1)}, bf16[128,128]{1,0:T(8,128)(2,1)}, u32[]{:S(2)}) copy-start(bf16[128,128]{1,0:T(8,128)(2,1)} %param.17) | copy-start | bytes 98308
  10.4 85.1 %copy-start.7 = (f32[2048]{0:T(1024)S(1)}, f32[2048]{0:T(1024)}, u32[]{:S(2)}) copy-start(f32[2048]{0:T(1024)} %param.26) | copy-start | bytes 24580
  104.0 15.2 %collective-permute-start = (f32[128,2048]{1,0:T(8,128)}, f32[128,2048]{1,0:T(8,128)S(1)}, u32[]{:S(2)}, u32[]{:S(2)}) collective-permute-start(f32[128,2048]{1,0:T(8,128)} %fusion.8), channel_id=1, source_target_pairs={{0,1},{1,0},{2,3},{3,2},{4,5},{5,4},{6,7},{7,6},{8,9},{9,8},{10,11... | collective-permute-start | bytes 3145736 | tf_op jit(solution)/shard_map/ppermute | solution.py:96
  120.6 14.9 %collective-permute-start.1 = (f32[128,2048]{1,0:T(8,128)S(1)}, f32[128,2048]{1,0:T(8,128)S(1)}, u32[]{:S(2)}, u32[]{:S(2)}) collective-permute-start(f32[128,2048]{1,0:T(8,128)S(1)} %add.101), channel_id=1, source_target_pairs={{0,2},{1,3},{2,0},{3,1},{4,6},{5,7},{6,4},{7,5},{8,10},{9,11},{10,... | collective-permute-start | bytes 3145736 | tf_op jit(solution)/shard_map/ppermute | solution.py:96
  135.6 51.6 %copy-start.5 = (f32[2048]{0:T(1024)S(1)}, f32[2048]{0:T(1024)}, u32[]{:S(2)}) copy-start(f32[2048]{0:T(1024)} %param.30) | copy-start | bytes 24580
  135.6 25.1 %collective-permute-start.2 = (f32[128,2048]{1,0:T(8,128)S(1)}, f32[128,2048]{1,0:T(8,128)S(1)}, u32[]{:S(2)}, u32[]{:S(2)}) collective-permute-start(f32[128,2048]{1,0:T(8,128)S(1)} %add.102), channel_id=1, source_target_pairs={{0,4},{1,5},{2,6},{3,7},{4,0},{5,1},{6,2},{7,3},{8,12},{9,13},{10,... | collective-permute-start | bytes 3145736 | tf_op jit(solution)/shard_map/ppermute | solution.py:96
  160.8 26.0 %collective-permute-start.3 = (f32[128,2048]{1,0:T(8,128)S(1)}, f32[128,2048]{1,0:T(8,128)S(1)}, u32[]{:S(2)}, u32[]{:S(2)}) collective-permute-start(f32[128,2048]{1,0:T(8,128)S(1)} %add.103), channel_id=1, source_target_pairs={{0,8},{1,9},{2,10},{3,11},{4,12},{5,13},{6,14},{7,15},{8,0},{9,1},... | collective-permute-start | bytes 3145736 | tf_op jit(solution)/shard_map/ppermute | solution.py:96
  187.2 14.4 %copy-start.2 = (s32[128]{0:T(128)S(1)}, s32[128]{0:T(128)}, u32[]{:S(2)}) copy-start(s32[128]{0:T(128)} %param.22) | copy-start | bytes 1540
  187.2 15.6 %copy-start.1 = (f32[128]{0:T(128)S(1)}, f32[128]{0:T(128)}, u32[]{:S(2)}) copy-start(f32[128]{0:T(128)} %param.23) | copy-start | bytes 1540
  201.5 3.8 %collective-permute-start.4 = (bf16[128,6400]{1,0:T(8,128)(2,1)}, bf16[128,6400]{1,0:T(8,128)(2,1)}, u32[]{:S(2)}, u32[]{:S(2)}) collective-permute-start(bf16[128,6400]{1,0:T(8,128)(2,1)} %get-tuple-element.14), channel_id=1, source_target_pairs={{0,16},{16,0},{1,17},{17,1},{2,18},{18,2},{3,19},{19,3},{4,20},{20... | collective-permute-start | bytes 4915208 | tf_op jit(solution)/shard_map/ppermute | solution.py:12
